TPU v7x, 32 devices: a whole 2x2x4 slice. The times are simulated.
32 devices in a mesh: groups: 2 (over x), inner: 16 (over z, y, core).
Axes of the slice: x: 2, y: 2, z: 4, core: 2. Of those that a mesh axis runs over, the one named last changes fastest.
Arguments:
- hidden_rows: bfloat16 [2048, 2048], P(('groups', 'inner')), parts along dimension 0, may hold values from -6 to 6
- token_embed: bfloat16 [2048, 2048], P(('groups', 'inner')), parts along dimension 0, may hold values from -6 to 6
- first_routes: int32 [2048, 8], P(('groups', 'inner')), parts along dimension 0, may hold values from 0 to 15, all different within a row; in each aligned block of 64 rows (0 to 63, 64 to 127, ...) at most 48 rows name the same one
- first_gates: float32 [2048, 8], P(('groups', 'inner')), parts along dimension 0, may hold values from 0.2 to 0.6
- first_gate_up: bfloat16 [16, 2048, 1024], P('inner'), may hold values from -0.125 to 0.125
- first_down: bfloat16 [16, 512, 2048], P('inner'), may hold values from -0.25 to 0.25
- second_routes: int32 [2048, 8], P(('groups', 'inner')), parts along dimension 0, may hold values from 0 to 15, all different within a row; in each aligned block of 64 rows (0 to 63, 64 to 127, ...) at most 48 rows name the same one
- second_gates: float32 [2048, 8], P(('groups', 'inner')), parts along dimension 0, may hold values from 0.2 to 0.6
- second_gate_up: bfloat16 [16, 2048, 1024], P('inner'), may hold values from -0.125 to 0.125
- second_down: bfloat16 [16, 512, 2048], P('inner'), may hold values from -0.25 to 0.25
- hidden_gain: float32 [2048], replicated, may hold values from 0.25 to 1.75
- embed_gain: float32 [2048], replicated, may hold values from 0.25 to 1.75
- merge_weight: bfloat16 [4096, 2048], P('inner'), may hold values from -0.09375 to 0.09375
Outputs:
- final_rows: bfloat16 [2048, 2048], P(('groups', 'inner')), parts along dimension 0
There are 2 independent parts, one for each index of `groups`. A program takes and returns all parts, laid end to end along the dimension named above; an argument that names none is the same for every part. Nothing has to cross between parts.
Inputs may be any that keep to these rules, and one draw needn't show every extreme that they name: `first_routes`: among the 64 tokens of one block, no expert is named more than 48 times, and in every draw some expert is named exactly 48 times in some block. `second_routes`: among the 64 tokens of one block, no expert is named more than 48 times, and in every draw some expert is named exactly 48 times in some block.
All inputs are finite; a program needn't handle non-finite values.
Results may differ from a plain program's by a relative error of at most 0.01.
Values may be sent and summed in bfloat16 or wider, within the bound.
A program may use at most 128 MiB of HBM per device.

v0:
```python
import functools

import jax
import jax.numpy as jnp
from jax import lax
from jax.experimental import pallas as pl
from jax.experimental.pallas import tpu as pltpu
from jax.sharding import PartitionSpec as P

EPSILON = 1e-06
LANES = 128
PARTS = 1
LAG = 0
VMEM_LIMIT = 60 * 1024 * 1024


class Ring:
    def __init__(self, devices, tok):
        self.devices, self.tok = devices, tok
        self.chips = devices // 2
        self.reach = self.chips // 2
        self.rise = self.chips // 2
        me = lax.axis_index("inner")
        chip = me // 2
        across = chip % 2
        along = chip // 2
        self.core = me % 2
        self.place = along * (1 - across) + (2 * self.rise - 1 - along) * across
        self.me = me

    def device(self, shift, other):
        place = (self.place + shift + self.chips) % self.chips
        across = place // self.rise
        along = place * (1 - across) + (2 * self.rise - 1 - place) * across
        core = self.core * (1 - other) + (1 - self.core) * other
        return (along * 2 + across) * 2 + core

    def row(self, way, distance, other):
        if distance == 0:
            return ((self.reach - 1) * 4 + 2 + other) * self.tok
        if distance == self.reach:
            return ((self.reach - 1) * 4 + other) * self.tok
        return ((distance - 1) * 4 + way * 2 + other) * self.tok

    def half(self, way, distance, other, k):
        part = self.tok // 2
        return pl.ds(self.row(way, distance, other) + k * part, part)

    def block(self, way, distance, other):
        return pl.ds(self.row(way, distance, other), self.tok)


def remote(src, dst, send, recv, device):
    return pltpu.make_async_remote_copy(
        src_ref=src, dst_ref=dst, send_sem=send, recv_sem=recv,
        device_id={"inner": device}, device_id_type=pl.DeviceIdType.MESH,
    )


def greet(devices):
    barrier = pltpu.get_barrier_semaphore()
    for device in devices:
        pl.semaphore_signal(
            barrier, inc=1, device_id={"inner": device}, device_id_type=pl.DeviceIdType.MESH
        )
    pl.semaphore_wait(barrier, len(devices))


def wide(values):
    return values.astype(jnp.float32)


def narrow(values):
    return values.astype(jnp.bfloat16)


class Reduce:
    def __init__(self, ring, bufs, part):
        share, paired, arrived, pair_send, pair_recv, send, recv = bufs
        self.ring, self.part = ring, part
        self.share, self.paired, self.arrived = share.at[part], paired.at[part], arrived.at[part]
        self.pair_send, self.pair_recv, self.send, self.recv = pair_send, pair_recv, send, recv
        self.started = []

    def slots(self, distance):
        return (0,) if distance in (0, self.ring.reach) else (0, 1)

    def pair_copy(self, way, distance):
        ring = self.ring
        slot = ring.reach * 2 if distance == 0 else (distance - 1) * 2 + way
        here = self.paired.at[pl.ds(slot * ring.tok, ring.tok)]
        return remote(
            self.share.at[ring.block(way, distance, 1)], here,
            self.pair_send.at[self.part, slot], self.pair_recv.at[self.part, slot],
            ring.device(0, 1),
        ), here

    def start_pair(self, distance):
        for way in self.slots(distance):
            copy, _ = self.pair_copy(way, distance)
            copy.start()
            self.started.append(copy)

    def finish_pair(self, distance):
        for way in self.slots(distance):
            copy, here = self.pair_copy(way, distance)
            copy.wait_recv()
            rows = self.ring.block(way, distance, 0)
            self.share[rows, :] = narrow(wide(self.share[rows, :]) + wide(here[...]))

    def hop(self, way, distance, k):
        ring = self.ring
        rows = ring.tok // 2
        slot = (way * ring.reach + distance - 1) * 2 + k
        landing = self.arrived.at[pl.ds(slot * rows, rows)]
        return remote(
            self.share.at[ring.half(1 - way, distance, 0, k)], landing,
            self.send.at[self.part, slot], self.recv.at[self.part, slot],
            ring.device(1 - 2 * way, 0),
        ), landing

    def start_hop(self, way, distance, k):
        copy, _ = self.hop(way, distance, k)
        copy.start()
        self.started.append(copy)

    def step(self, way, distance, k):
        copy, landing = self.hop(way, distance + 1, k)
        copy.wait_recv()
        rows = self.ring.half(1 - way, distance, 0, k)
        self.share[rows, :] = narrow(wide(self.share[rows, :]) + wide(landing[...]))
        self.start_hop(way, distance, k)

    def early(self):
        reach = self.ring.reach
        if reach > 1:
            for way in (0, 1):
                self.start_hop(way, reach - 1, 1 - way)

    def late(self):
        for way in (0, 1):
            self.start_hop(way, self.ring.reach, way)

    def run(self):
        reach = self.ring.reach
        for distance in range(reach - 1, 0, -1):
            yield
            for way in (0, 1):
                self.step(way, distance, way)
            if distance > 1:
                for way in (0, 1):
                    self.step(way, distance - 1, 1 - way)
        yield
        totals = []
        for k in (0, 1):
            total = wide(self.share[self.ring.half(0, 0, 0, k), :])
            for way in (0, 1):
                if k == way or reach > 1:
                    copy, landing = self.hop(way, 1, k)
                    copy.wait_recv()
                    total = total + wide(landing[...])
            totals.append(total)
        return jnp.concatenate(totals, axis=0)


def reduce_scratch(devices, tok, width):
    reach = devices // 4
    return [
        pltpu.VMEM((PARTS, devices * tok, width), jnp.bfloat16),
        pltpu.VMEM((PARTS, (2 * reach + 1) * tok, width), jnp.bfloat16),
        pltpu.VMEM((PARTS, 2 * reach * tok, width), jnp.bfloat16),
        pltpu.SemaphoreType.DMA((PARTS, 2 * reach + 1)),
        pltpu.SemaphoreType.DMA((PARTS, 2 * reach + 1)),
        pltpu.SemaphoreType.DMA((PARTS, 4 * reach)),
        pltpu.SemaphoreType.DMA((PARTS, 4 * reach)),
    ]


def gather_scratch(devices, tok, width):
    reach = devices // 4
    return [
        pltpu.VMEM((PARTS, devices * tok, width), jnp.bfloat16),
        pltpu.SemaphoreType.DMA((PARTS, 4 * reach)),
        pltpu.SemaphoreType.DMA((PARTS, 4 * reach)),
        pltpu.SemaphoreType.DMA((PARTS, 4 * reach + 1)),
        pltpu.SemaphoreType.DMA((PARTS, 4 * reach + 1)),
    ]


def normed(values, gain):
    widened = wide(values)
    inverse_rms = lax.rsqrt(jnp.mean(widened * widened, axis=-1, keepdims=True) + EPSILON)
    return narrow(widened * inverse_rms * gain)


def gate_lanes(devices, lanes, tables):
    rows = tables[0][0].shape[0]
    lane = lax.broadcasted_iota(jnp.int32, (rows, lanes), 1)
    packed = jnp.zeros((rows, lanes), jnp.float32)
    for layer, (routes, gates) in enumerate(tables):
        base = 2 * layer * devices
        high_part = (lane >= base) & (lane < base + devices)
        low_part = (lane >= base + devices) & (lane < base + 2 * devices)
        expert = jnp.where(high_part, lane - base, lane - base - devices)
        dense = jnp.zeros((rows, lanes), jnp.float32)
        for k in range(routes.shape[1]):
            dense = dense + jnp.where(expert == routes[:, k : k + 1], gates[:, k : k + 1], 0.0)
        high = wide(narrow(dense))
        packed = jnp.where(high_part, high, jnp.where(low_part, dense - high, packed))
    return narrow(packed)


def block_kernel(devices, *refs):
    (hidden_ref, embed_ref, routes1, gates1, routes2, gates2, hidden_gain, embed_gain,
     gu1_ref, down1_ref, weight_ref, gu2_ref, down2_ref, out_ref) = refs[:14]
    scratch = list(refs[14:])
    take = lambda count: [scratch.pop(0) for _ in range(count)]
    gu1, down1, weight, gu2, down2, load_sem = take(6)
    packed, after_first, after_merge, pieces, columns, inner = take(6)
    piece_send, piece_recv, own_sem = take(3)
    gather1, gather2 = take(5), take(5)
    reduce1, reduce2, reduce3 = take(7), take(7), take(7)
    rows_all, width = hidden_ref.shape
    tok = rows_all // PARTS
    hidden = down1.shape[0]
    depth = weight.shape[0]
    lanes = packed.shape[1] - width
    ring = Ring(devices, tok)
    reach = ring.reach

    loads = [
        pltpu.make_async_copy(source, target, load_sem.at[i])
        for i, (source, target) in enumerate(
            [(gu1_ref.at[0], gu1), (down1_ref.at[0], down1), (weight_ref, weight),
             (gu2_ref.at[0], gu2), (down2_ref.at[0], down2)]
        )
    ]
    for load in loads:
        load.start()
    waiting = list(range(5))

    def need(*which):
        for i in which:
            if i in waiting:
                waiting.remove(i)
                loads[i].wait()

    packed[:, :width] = hidden_ref[...]
    packed[:, width:] = gate_lanes(
        devices, lanes, [(routes1[...], gates1[...]), (routes2[...], gates2[...])]
    )

    partners = [(0, 0, 1)]
    for distance in range(1, reach + 1):
        for other in (0, 1):
            partners.append((0, distance, other))
            if distance < reach:
                partners.append((1, distance, other))

    def target_of(way, distance, other):
        return ring.device(distance * (1 - 2 * way), other)

    greet([target_of(*partner) for partner in partners])
    started = []

    def begin(copy):
        copy.start()
        started.append(copy)

    def layer(part, source, bufs, first, reduce_bufs, load_ids, gu, down):
        everyone, send, recv, sib_send, sib_recv = bufs
        everyone = everyone.at[part]
        own_rows = pl.ds(part * tok, tok)

        def ring_copy(way, distance, k):
            slot = (way * reach + distance - 1) * 2 + k
            landing = everyone.at[ring.half(way, distance, 0, k)]
            origin = (
                source.at[pl.ds(part * tok + k * (tok // 2), tok // 2)]
                if distance == 1
                else everyone.at[ring.half(way, distance - 1, 0, k)]
            )
            return remote(
                origin, landing, send.at[part, slot], recv.at[part, slot],
                ring.device(1 - 2 * way, 0),
            )

        def sibling_copy(way, distance, k):
            if distance == 0:
                slot, origin, landing = 4 * reach, source.at[own_rows], everyone.at[ring.block(0, 0, 1)]
            else:
                slot = (way * reach + distance - 1) * 2 + k
                origin = everyone.at[ring.half(way, distance, 0, k)]
                landing = everyone.at[ring.half(way, distance, 1, k)]
            return remote(
                origin, landing, sib_send.at[part, slot], sib_recv.at[part, slot],
                ring.device(0, 1),
            )

        reducing = Reduce(ring, reduce_bufs, part)
        share = reducing.share
        gate_rows = gather1[0].at[part]

        def span_of(distance):
            if distance == 0:
                return ring.row(0, 0, 0), 2 * tok
            return (distance - 1) * 4 * tok, (2 if distance == reach else 4) * tok

        def up(distance):
            first_row, count = span_of(distance)
            rows = pl.ds(first_row, count)
            step = min(256, hidden)

            @pl.loop(0, hidden // step)
            def _(j):
                left = pl.ds(pl.multiple_of(j * step, step), step)
                right = pl.ds(pl.multiple_of(hidden + j * step, step), step)
                x = everyone[rows, :width]
                g = jnp.dot(x, gu[:, left], preferred_element_type=jnp.float32)
                u = jnp.dot(x, gu[:, right], preferred_element_type=jnp.float32)
                inner[part, :count, left] = narrow(jax.nn.silu(g) * u)

        def finish(distance):
            first_row, count = span_of(distance)
            rows = pl.ds(first_row, count)
            lane = lax.broadcasted_iota(jnp.int32, (count, lanes), 1)
            mine = (lane == ring.me + first * devices) | (lane == ring.me + (first + 1) * devices)
            gate = jnp.sum(
                jnp.where(mine, wide(gate_rows[rows, width:]), 0.0), axis=1, keepdims=True
            )
            span = min(512, width)

            @pl.loop(0, width // span)
            def _(j):
                cut = pl.ds(pl.multiple_of(j * span, span), span)
                out = jnp.dot(
                    inner[part, :count, :], down[:, cut], preferred_element_type=jnp.float32
                )
                share[rows, cut] = narrow(out * gate)

            reducing.start_pair(distance)

        def streams(distance):
            for short in (0, 1):
                if not (short and distance == reach):
                    for way in (0, 1):
                        yield way, (1 - way if short else way), short

        for way, k, _ in streams(1):
            begin(ring_copy(way, 1, k))
        begin(sibling_copy(0, 0, 0))
        everyone[ring.block(0, 0, 0), :] = source[own_rows, :]

        def pass_on(distance, short):
            for way, k, which in streams(distance):
                if which == short:
                    ring_copy(way, distance, k).wait_recv()
                    if distance < reach and not (short and distance == reach - 1):
                        begin(ring_copy(way, distance + 1, k))
                    begin(sibling_copy(way, distance, k))

        def from_sibling(distance):
            if distance == 0:
                sibling_copy(0, 0, 0).wait_recv()
            else:
                for way, k, _ in streams(distance):
                    sibling_copy(way, distance, k).wait_recv()

        yield
        need(*load_ids)
        from_sibling(0)
        up(0)
        for distance in range(1, reach):
            yield
            pass_on(distance, 0)
            if distance == 1:
                finish(0)
            else:
                from_sibling(distance - 1)
                up(distance - 1)
            yield
            pass_on(distance, 1)
            if distance > 1:
                finish(distance - 1)
                reducing.finish_pair(distance - 2)
        yield
        if reach > 1:
            from_sibling(reach - 1)
            up(reach - 1)
        yield
        pass_on(reach, 0)
        if reach > 1:
            finish(reach - 1)
            reducing.finish_pair(reach - 2)
        yield
        from_sibling(reach)
        up(reach)
        if reach > 1:
            reducing.finish_pair(reach - 1)
            reducing.early()
        finish(reach)
        yield
        reducing.finish_pair(reach)
        reducing.late()
        total = yield from reducing.run()
        started.extend(reducing.started)
        return total

    def merged(part):
        here, landed = pieces.at[part], columns.at[part]

        def piece(way, distance, other):
            target = target_of(way, distance, other)
            slot = ring.row(way, distance, other) // tok
            return remote(
                here.at[target], landed.at[ring.block(way, distance, other)],
                piece_send.at[part, slot], piece_recv.at[part, slot], target,
            )

        for partner in reversed(partners):
            begin(piece(*partner))
        own = pltpu.make_async_copy(
            here.at[ring.me], landed.at[ring.block(0, 0, 0)], own_sem.at[part]
        )
        own.start()
        need(2)
        reducing = Reduce(ring, reduce2, part)
        share = reducing.share
        for distance in range(reach, 0, -1):
            if distance % 2 == 0:
                yield
            if distance == reach:
                own.wait()
            for way, far, other in partners:
                if far == distance or (far == 0 and distance == reach):
                    piece(way, far, other).wait_recv()
            rows = pl.ds((distance - 1) * 4 * tok, 4 * tok)
            span = min(512, width)

            @pl.loop(0, width // span)
            def _(j):
                cut = pl.ds(pl.multiple_of(j * span, span), span)
                share[rows, cut] = narrow(
                    jnp.dot(landed[rows, :], weight[:, cut], preferred_element_type=jnp.float32)
                )

            reducing.start_pair(distance)
            if distance == reach:
                reducing.start_pair(0)
                reducing.finish_pair(reach)
                reducing.late()
                reducing.finish_pair(0)
            else:
                reducing.finish_pair(distance)
                if distance == reach - 1:
                    reducing.early()
        total = yield from reducing.run()
        started.extend(reducing.started)
        return total

    def scatter_pieces(part, values, at):
        for j in range(width // depth):
            pieces[part, at + j] = values[:, j * depth : (j + 1) * depth]

    def pipeline(part):
        rows = pl.ds(part * tok, tok)
        total = yield from layer(part, packed, gather1, 0, reduce1, (0, 1), gu1, down1)
        first = narrow(wide(hidden_ref[rows, :]) + total)
        after_first[rows, :] = first
        scatter_pieces(part, normed(first, hidden_gain[...]), 0)
        total = yield from merged(part)
        after_merge[rows, :] = narrow(wide(after_first[rows, :]) + jax.nn.silu(total))
        total = yield from layer(part, after_merge, gather2, 2, reduce3, (3, 4), gu2, down2)
        out_ref[rows, :] = narrow(wide(after_merge[rows, :]) + total)

    lines = [pipeline(part) for part in range(PARTS)]
    done = object()
    tick = 0
    while lines:
        for at, line in enumerate(list(lines)):
            if tick >= at * LAG or len(lines) < PARTS:
                if next(line, done) is done:
                    lines.remove(line)
        if tick == 0:
            for part in range(PARTS):
                rows = pl.ds(part * tok, tok)
                scatter_pieces(part, normed(embed_ref[rows, :], embed_gain[...]), width // depth)
        tick += 1
    for copy in started:
        copy.wait_send()


def fused(hidden_rows, token_embed, first_routes, first_gates, first_gate_up, first_down,
          second_routes, second_gates, second_gate_up, second_down, hidden_gain, embed_gain,
          merge_weight):
    devices = lax.axis_size("inner")
    rows, width = hidden_rows.shape
    tok = rows // PARTS
    hidden = first_down.shape[1]
    depth = merge_weight.shape[0]
    lanes = -(-4 * devices // LANES) * LANES
    vmem = pl.BlockSpec(memory_space=pltpu.VMEM)
    hbm = pl.BlockSpec(memory_space=pl.ANY)
    bf16 = jnp.bfloat16
    scratch = [
        pltpu.VMEM(first_gate_up.shape[1:], bf16),
        pltpu.VMEM(first_down.shape[1:], bf16),
        pltpu.VMEM(merge_weight.shape, bf16),
        pltpu.VMEM(second_gate_up.shape[1:], bf16),
        pltpu.VMEM(second_down.shape[1:], bf16),
        pltpu.SemaphoreType.DMA((5,)),
        pltpu.VMEM((rows, width + lanes), bf16),
        pltpu.VMEM((rows, width), bf16),
        pltpu.VMEM((rows, width), bf16),
        pltpu.VMEM((PARTS, devices, tok, depth), bf16),
        pltpu.VMEM((PARTS, devices * tok, depth), bf16),
        pltpu.VMEM((PARTS, 4 * tok, hidden), bf16),
        pltpu.SemaphoreType.DMA((PARTS, devices)),
        pltpu.SemaphoreType.DMA((PARTS, devices)),
        pltpu.SemaphoreType.DMA((PARTS,)),
    ]
    scratch += gather_scratch(devices, tok, width + lanes) + gather_scratch(devices, tok, width)
    for _ in range(3):
        scratch += reduce_scratch(devices, tok, width)
    return pl.pallas_call(
        functools.partial(block_kernel, devices),
        out_shape=jax.ShapeDtypeStruct((rows, width), bf16),
        in_specs=[vmem] * 8 + [hbm] * 5,
        out_specs=vmem,
        scratch_shapes=scratch,
        compiler_params=pltpu.CompilerParams(
            collective_id=0, has_side_effects=True, vmem_limit_bytes=VMEM_LIMIT
        ),
    )(hidden_rows, token_embed, first_routes, first_gates, second_routes, second_gates,
      hidden_gain[None], embed_gain[None], first_gate_up, first_down, merge_weight,
      second_gate_up, second_down)


def rms_scale(values, gain_vec):
    widened = values.astype(jnp.float32)
    inverse_rms = lax.rsqrt(jnp.mean(widened * widened, axis=-1, keepdims=True) + EPSILON)
    return (widened * inverse_rms * gain_vec).astype(jnp.bfloat16)


def dense_gates(routes, gates, experts):
    hit = routes[:, :, None] == jnp.arange(experts, dtype=jnp.int32)[None, None, :]
    return jnp.sum(jnp.where(hit, gates[:, :, None], 0.0), axis=1)


def plain_layer(devices, rows, routes, gates, gate_up, down):
    dense = lax.all_gather(dense_gates(routes, gates, devices), "inner", axis=0, tiled=True)
    column = lax.dynamic_slice_in_dim(dense, lax.axis_index("inner"), 1, axis=1)
    everyone = lax.all_gather(rows, "inner", axis=0, tiled=True)
    width = down.shape[1]
    projected = jnp.dot(everyone, gate_up[0], preferred_element_type=jnp.float32)
    inner = narrow(jax.nn.silu(projected[:, :width]) * projected[:, width:])
    share = narrow(jnp.dot(inner, down[0], preferred_element_type=jnp.float32) * column)
    total = lax.psum_scatter(share, "inner", scatter_dimension=0, tiled=True)
    return narrow(wide(rows) + wide(total))


def plain_merge(after_first, merged_in, weight):
    columns = lax.all_to_all(merged_in, "inner", split_axis=1, concat_axis=0, tiled=True)
    partial = narrow(jnp.dot(columns, weight, preferred_element_type=jnp.float32))
    merged = lax.psum_scatter(partial, "inner", scatter_dimension=0, tiled=True)
    return narrow(wide(after_first) + jax.nn.silu(wide(merged)))


def unfused(hidden_rows, token_embed, first_routes, first_gates, first_gate_up, first_down,
            second_routes, second_gates, second_gate_up, second_down, hidden_gain, embed_gain,
            merge_weight):
    devices = lax.axis_size("inner")
    after_first = plain_layer(
        devices, hidden_rows, first_routes, first_gates, first_gate_up, first_down
    )
    merged_in = jnp.concatenate(
        [rms_scale(after_first, hidden_gain), rms_scale(token_embed, embed_gain)], axis=1
    )
    after_merge = plain_merge(after_first, merged_in, merge_weight)
    return plain_layer(devices, after_merge, second_routes, second_gates, second_gate_up, second_down)


def local(hidden_rows, *others):
    devices = lax.axis_size("inner")
    tok, width = hidden_rows.shape
    fits = 12 * devices * tok * width * 2 <= VMEM_LIMIT and devices % 4 == 0 and tok % 32 == 0
    return (fused if fits else unfused)(hidden_rows, *others)


def solution(mesh):
    rows = P(("groups", "inner"), None)
    return jax.shard_map(
        local,
        mesh=mesh,
        in_specs=(
            rows, rows, rows, rows,
            P("inner", None, None),
            P("inner", None, None),
            rows, rows,
            P("inner", None, None),
            P("inner", None, None),
            P(),
            P(),
            P("inner", None),
        ),
        out_specs=rows,
        check_vma=False,
    )
```

profile of v0, /device:TPU:0, one launch (start us, length us, event | category | flops | bytes accessed | tf_op | source)
XLA Modules:
  0.0 153.4 jit_solution(2331287693861512776)
XLA Ops:
  0.0 1.4 copy.14.refs_2_
  1.4 1.4 copy.15.refs_3_
  2.8 1.4 copy.16.refs_4_
  4.1 1.4 copy.17.refs_5_
  5.5 146.3 %shard_map.127 = bf16[64,2048]{1,0:T(8,128)(2,1)} custom-call(bf16[64,2048]{1,0:T(8,128)(2,1)} %refs_0_.1, bf16[64,2048]{1,0:T(8,128)(2,1)} %refs_1_.1, s32[64,8]{1,0:T(8,128)} %copy.14.refs_2_, f32[64,8]{1,0:T(8,128)} %copy.15.refs_3_, s32[64,8]{1,0:T(8,128)} %copy.16.refs_4_, f32[64,8]{1,0:T(8,128)} %copy.17.refs_5_, f32[1,2048]{1,0:T(1,128)} %bitcast.2, ...), custom_call_target="tpu_custom_call" | custom-call | tf_op jit(solution)/shard_map/pallas_call | solution.py:525
  151.8 1.7 %copy.19 = bf16[64,2048]{1,0:T(8,128)(2,1)} copy(bf16[64,2048]{1,0:T(8,128)(2,1)} %shard_map.127) | data formatting | bytes 524288
where the time goes:
time: 154 us; the launch traced here: 153 us
  Pallas kernels  146 us (95%)
  local copies, waits for them, and re-layouts  7.17 us (5%)
    pallas_call x1, Pallas kernels, fused(): pl.pallas_call(functools.partial(block_kernel, devices), out_shape=jax.Sh...  146 us
    unnamed x5, local copies, waits for them, and re-layouts  7.17 us

commit v1 on v0

v1 whole, which is shorter than its diff:
```python
import functools

import jax
import jax.numpy as jnp
from jax import lax
from jax.experimental import pallas as pl
from jax.experimental.pallas import tpu as pltpu
from jax.sharding import PartitionSpec as P

EPSILON = 1e-06
LANES = 128
CUTS = 2
VMEM_LIMIT = 60 * 1024 * 1024


class Ring:
    def __init__(self, devices, tok):
        self.devices, self.tok = devices, tok
        self.chips = devices // 2
        self.reach = self.chips // 2
        self.rise = self.chips // 2
        me = lax.axis_index("inner")
        chip = me // 2
        across = chip % 2
        along = chip // 2
        self.core = me % 2
        self.place = along * (1 - across) + (2 * self.rise - 1 - along) * across
        self.me = me
        self.spans = [(0, 0)]
        for distance in range(1, self.reach):
            self.spans += [(distance, 0), (distance, 1)]
        self.spans.append((self.reach, 0))

    def device(self, shift, other):
        place = (self.place + shift + self.chips) % self.chips
        across = place // self.rise
        along = place * (1 - across) + (2 * self.rise - 1 - place) * across
        core = self.core * (1 - other) + (1 - self.core) * other
        return (along * 2 + across) * 2 + core

    def first(self, distance, s):
        if distance == 0:
            return ((self.reach - 1) * 4 + 2) * self.tok
        return ((distance - 1) * 4 + 2 * s) * self.tok

    def rows(self, distance, s):
        return pl.ds(self.first(distance, s), 2 * self.tok)

    def side(self, distance, s, other):
        return pl.ds(self.first(distance, s) + other * self.tok, self.tok)

    def half(self, way, distance, other, k):
        part = self.tok // 2
        if distance == 0:
            s, column = 0, k
        elif distance == self.reach:
            s, column = 0, k
        else:
            s, column = (0 if k == way else 1), way
        return pl.ds(self.first(distance, s) + other * self.tok + column * part, part)

    def slot(self, way, distance, other):
        if distance == 0:
            return (self.reach - 1) * 4 + 2 + other
        if distance == self.reach:
            return (self.reach - 1) * 4 + other
        return (distance - 1) * 4 + way * 2 + other


def remote(src, dst, send, recv, device):
    return pltpu.make_async_remote_copy(
        src_ref=src, dst_ref=dst, send_sem=send, recv_sem=recv,
        device_id={"inner": device}, device_id_type=pl.DeviceIdType.MESH,
    )


def wide(values):
    return values.astype(jnp.float32)


def narrow(values):
    return values.astype(jnp.bfloat16)


class Reduce:
    def __init__(self, ring, bufs, started):
        self.ring, self.started = ring, started
        (self.share, self.paired, self.arrived, self.pair_send, self.pair_recv, self.send,
         self.recv) = bufs
        self.cut = self.share.shape[1] // CUTS

    def pair_copy(self, distance, s):
        ring = self.ring
        slot = ring.spans.index((distance, s))
        here = self.paired.at[pl.ds(slot * ring.tok, ring.tok)]
        return remote(
            self.share.at[ring.side(distance, s, 1)], here,
            self.pair_send.at[slot], self.pair_recv.at[slot], ring.device(0, 1),
        ), here

    def begin(self, copy):
        copy.start()
        self.started.append(copy)

    def start_pair(self, distance, s):
        self.begin(self.pair_copy(distance, s)[0])

    def finish_pair(self, distance, s):
        copy, here = self.pair_copy(distance, s)
        copy.wait_recv()
        rows = self.ring.side(distance, s, 0)
        self.share[rows, :] = narrow(wide(self.share[rows, :]) + wide(here[...]))

    def columns(self, c):
        return pl.ds(c * self.cut, self.cut)

    def hop(self, way, distance, k, c):
        ring = self.ring
        rows = ring.tok // 2
        slot = (way * ring.reach + distance - 1) * 2 + k
        landing = self.arrived.at[pl.ds(slot * rows, rows), self.columns(c)]
        return remote(
            self.share.at[ring.half(1 - way, distance, 0, k), self.columns(c)], landing,
            self.send.at[slot * CUTS + c], self.recv.at[slot * CUTS + c],
            ring.device(1 - 2 * way, 0),
        ), landing

    def launch(self, distance, flip):
        for c in range(CUTS):
            for way in (0, 1):
                self.begin(self.hop(way, distance, 1 - way if flip else way, c)[0])

    def step(self, distance, flip):
        for c in range(CUTS):
            for way in (0, 1):
                k = 1 - way if flip else way
                copy, landing = self.hop(way, distance + 1, k, c)
                copy.wait_recv()
                at = (self.ring.half(1 - way, distance, 0, k), self.columns(c))
                self.share[at] = narrow(wide(self.share[at]) + wide(landing[...]))
                self.begin(self.hop(way, distance, k, c)[0])

    def total(self):
        parts = []
        for c in range(CUTS):
            halves = []
            for k in (0, 1):
                piece = wide(self.share[self.ring.half(0, 0, 0, k), self.columns(c)])
                for way in (0, 1):
                    copy, landing = self.hop(way, 1, k, c)
                    copy.wait_recv()
                    piece = piece + wide(landing[...])
                halves.append(piece)
            parts.append(jnp.concatenate(halves, axis=0))
        return jnp.concatenate(parts, axis=1)


def reduce_scratch(devices, tok, width):
    reach = devices // 4
    return [
        pltpu.VMEM((devices * tok, width), jnp.bfloat16),
        pltpu.VMEM((2 * reach * tok, width), jnp.bfloat16),
        pltpu.VMEM((2 * reach * tok, width), jnp.bfloat16),
        pltpu.SemaphoreType.DMA((2 * reach,)),
        pltpu.SemaphoreType.DMA((2 * reach,)),
        pltpu.SemaphoreType.DMA((4 * reach * CUTS,)),
        pltpu.SemaphoreType.DMA((4 * reach * CUTS,)),
    ]


def gather_scratch(devices, tok, width):
    reach = devices // 4
    return [
        pltpu.VMEM((devices * tok, width), jnp.bfloat16),
        pltpu.SemaphoreType.DMA((4 * reach,)),
        pltpu.SemaphoreType.DMA((4 * reach,)),
        pltpu.SemaphoreType.DMA((4 * reach + 1,)),
        pltpu.SemaphoreType.DMA((4 * reach + 1,)),
    ]


def normed(values, gain):
    widened = wide(values)
    inverse_rms = lax.rsqrt(jnp.mean(widened * widened, axis=-1, keepdims=True) + EPSILON)
    return narrow(widened * inverse_rms * gain)


def gate_lanes(devices, turned, tables):
    rows = tables[0][0].shape[1]
    turned[...] = jnp.zeros_like(turned)
    for layer, (routes, gates) in enumerate(tables):
        base = 2 * layer * devices
        expert = lax.broadcasted_iota(jnp.int32, (devices, rows), 0)
        dense = jnp.zeros((devices, rows), jnp.float32)
        for k in range(routes.shape[0]):
            dense = dense + jnp.where(expert == routes[k : k + 1, :], gates[k : k + 1, :], 0.0)
        high = wide(narrow(dense))
        turned[base : base + devices, :rows] = high
        turned[base + devices : base + 2 * devices, :rows] = dense - high
    return narrow(turned[...].T[:rows, :])


def block_kernel(devices, *refs):
    (routes1, gates1, routes2, gates2, hidden_gain, embed_gain, hidden_ref, embed_ref,
     gu1_ref, down1_ref, weight_ref, gu2_ref, down2_ref, out_ref) = refs[:14]
    scratch = list(refs[14:])
    take = lambda count: [scratch.pop(0) for _ in range(count)]
    gu1, down1, weight, gu2, down2, load_sem = take(6)
    turned, embed, after_first, pieces, landed, inner = take(6)
    piece_send, piece_recv, own_sem, lane_send, lane_pair = take(5)
    gather1, gather2 = take(5), take(5)
    reduce1, reduce2, reduce3 = take(7), take(7), take(7)
    tok, width = hidden_ref.shape
    hidden = down1.shape[0]
    depth = weight.shape[0]
    lanes = gather1[0].shape[1] - width
    ring = Ring(devices, tok)
    reach = ring.reach
    part = tok // 2

    barrier = pltpu.get_barrier_semaphore()
    neighbours = [ring.device(1, 0), ring.device(-1, 0), ring.device(0, 1)]
    for device in neighbours:
        pl.semaphore_signal(
            barrier, inc=1, device_id={"inner": device}, device_id_type=pl.DeviceIdType.MESH
        )
    own_rows = ring.side(0, 0, 0)
    loads = [
        pltpu.make_async_copy(source, target, load_sem.at[i])
        for i, (source, target) in enumerate(
            [(hidden_ref, gather1[0].at[own_rows, pl.ds(0, width)]), (embed_ref, embed),
             (gu1_ref.at[0], gu1), (down1_ref.at[0], down1), (weight_ref, weight),
             (gu2_ref.at[0], gu2), (down2_ref.at[0], down2)]
        )
    ]
    waiting = list(range(len(loads)))

    def need(*which):
        for i in which:
            if i in waiting:
                waiting.remove(i)
                loads[i].wait()

    pl.semaphore_wait(barrier, len(neighbours))
    started = []

    def begin(copy):
        copy.start()
        started.append(copy)

    partners = [(0, 0, 1)]
    for distance in range(1, reach + 1):
        for other in (0, 1):
            partners.append((0, distance, other))
            if distance < reach:
                partners.append((1, distance, other))

    def streams(s):
        return [(way, 1 - way if s else way) for way in (0, 1)]

    def ring_copy(bufs, way, distance, k):
        everyone, send, recv = bufs[:3]
        slot = (way * reach + distance - 1) * 2 + k
        if distance == 1:
            origin = everyone.at[ring.half(way, 0, 0, k)]
        else:
            origin = everyone.at[ring.half(way, distance - 1, 0, k)]
        return remote(
            origin, everyone.at[ring.half(way, distance, 0, k)], send.at[slot], recv.at[slot],
            ring.device(1 - 2 * way, 0),
        )

    def sibling_copy(bufs, way, distance, k):
        everyone, sib_send, sib_recv = bufs[0], bufs[3], bufs[4]
        if distance == 0:
            slot, origin, landing = 4 * reach, own_rows, ring.side(0, 0, 1)
        else:
            slot = (way * reach + distance - 1) * 2 + k
            origin, landing = ring.half(way, distance, 0, k), ring.half(way, distance, 1, k)
        return remote(
            everyone.at[origin], everyone.at[landing], sib_send.at[slot], sib_recv.at[slot],
            ring.device(0, 1),
        )

    def first_sends():
        everyone, send, recv, sib_send, sib_recv = gather1
        narrow_cut, lane_cut = pl.ds(0, width), pl.ds(width, lanes)

        def send_rows(way, k):
            slot = way * reach * 2 + k
            return remote(
                hidden_ref.at[pl.ds(k * part, part)],
                everyone.at[ring.half(way, 1, 0, k), narrow_cut],
                send.at[slot], recv.at[slot], ring.device(1 - 2 * way, 0),
            )

        def send_lanes(way, k):
            slot = way * reach * 2 + k
            return remote(
                everyone.at[ring.half(way, 0, 0, k), lane_cut],
                everyone.at[ring.half(way, 1, 0, k), lane_cut],
                lane_send.at[way * 2 + k], recv.at[slot], ring.device(1 - 2 * way, 0),
            )

        for way, k in streams(0):
            begin(send_rows(way, k))
        begin(remote(
            hidden_ref, everyone.at[ring.side(0, 0, 1), narrow_cut],
            sib_send.at[4 * reach], sib_recv.at[4 * reach], ring.device(0, 1),
        ))
        for load in loads:
            load.start()
        everyone[own_rows, lane_cut] = gate_lanes(
            devices, turned, [(routes1[...], gates1[...]), (routes2[...], gates2[...])]
        )
        for way, k in streams(0):
            begin(send_lanes(way, k))
        begin(remote(
            everyone.at[own_rows, lane_cut], everyone.at[ring.side(0, 0, 1), lane_cut],
            lane_pair.at[0], sib_recv.at[4 * reach], ring.device(0, 1),
        ))
        for way, k in streams(1):
            begin(send_rows(way, k))
            begin(send_lanes(way, k))

    def layer(bufs, first, reducing, load_ids, gu, down, meanwhile):
        everyone = bufs[0]
        share = reducing.share
        gate_rows = gather1[0]
        step = min(256, hidden)
        steps = hidden // step

        def pass_on(distance, s):
            for way, k in streams(s):
                ring_copy(bufs, way, distance, k).wait_recv()
                if distance + 1 < reach or (distance + 1 == reach and s == 0):
                    begin(ring_copy(bufs, way, distance + 1, k))
                begin(sibling_copy(bufs, way, distance, k))

        def from_sibling(distance, s):
            if distance == 0:
                sibling_copy(bufs, 0, 0, 0).wait_recv()
            else:
                for way, k in streams(s):
                    sibling_copy(bufs, way, distance, k).wait_recv()

        def up(first_row, count, low, high):
            rows = pl.ds(first_row, count)

            @pl.loop(low, high)
            def _(j):
                left = pl.ds(pl.multiple_of(j * step, step), step)
                right = pl.ds(pl.multiple_of(hidden + j * step, step), step)
                x = everyone[rows, :width]
                g = jnp.dot(x, gu[:, left], preferred_element_type=jnp.float32)
                u = jnp.dot(x, gu[:, right], preferred_element_type=jnp.float32)
                inner[:count, left] = narrow(jax.nn.silu(g) * u)

        def finish(first_row, count, *spans):
            rows = pl.ds(first_row, count)
            lane = lax.broadcasted_iota(jnp.int32, (count, lanes), 1)
            mine = (lane == ring.me + first * devices) | (lane == ring.me + (first + 1) * devices)
            gate = jnp.sum(
                jnp.where(mine, wide(gate_rows[rows, width:]), 0.0), axis=1, keepdims=True
            )
            span = min(512, width)

            @pl.loop(0, width // span)
            def _(j):
                cut = pl.ds(pl.multiple_of(j * span, span), span)
                out = jnp.dot(
                    inner[:count, :], down[:, cut], preferred_element_type=jnp.float32
                )
                share[rows, cut] = narrow(out * gate)

            for at in spans:
                reducing.start_pair(*at)

        near = ring.first(0, 0)
        from_sibling(0, 0)
        need(load_ids[0])
        up(near, 2 * tok, 0, steps)
        need(load_ids[1])
        finish(near, 2 * tok, (0, 0))
        meanwhile()
        pass_on(1, 0)
        for distance in range(1, reach - 1):
            pass_on(distance, 1)
            from_sibling(distance, 0)
            from_sibling(distance, 1)
            up(ring.first(distance, 0), 4 * tok, 0, steps // 2)
            pass_on(distance + 1, 0)
            up(ring.first(distance, 0), 4 * tok, steps // 2, steps)
            finish(ring.first(distance, 0), 4 * tok, (distance, 0), (distance, 1))
            if distance == 1:
                reducing.finish_pair(0, 0)
            else:
                reducing.finish_pair(distance - 1, 0)
                reducing.finish_pair(distance - 1, 1)
        last = reach - 1
        pass_on(last, 1)
        from_sibling(last, 0)
        up(ring.first(last, 0), 2 * tok, 0, steps)
        finish(ring.first(last, 0), 2 * tok, (last, 0))
        pass_on(reach, 0)
        from_sibling(last, 1)
        reducing.finish_pair(last, 0)
        reducing.launch(last, True)
        from_sibling(reach, 0)
        up(ring.first(last, 1), 4 * tok, 0, steps)
        finish(ring.first(last, 1), 4 * tok, (reach, 0), (last, 1))
        reducing.finish_pair(last - 1, 0)
        reducing.finish_pair(last - 1, 1)
        reducing.step(last - 1, True)
        reducing.finish_pair(reach, 0)
        reducing.launch(reach, False)
        reducing.finish_pair(last, 1)
        for distance in range(last, 0, -1):
            if distance > 2:
                reducing.step(distance - 2, True)
            reducing.step(distance, False)

    def target_of(way, distance, other):
        return ring.device(distance * (1 - 2 * way), other)

    def piece(way, distance, other):
        target = target_of(way, distance, other)
        slot = ring.slot(way, distance, other)
        return remote(
            pieces.at[target], landed.at[pl.ds(slot * tok, tok)],
            piece_send.at[slot], piece_recv.at[slot], target,
        ), target * depth >= width

    def send_pieces(late):
        for partner in reversed(partners):
            copy, embedded = piece(*partner)

            @pl.when(embedded if late == 0 else jnp.logical_not(embedded))
            def _():
                copy.start()

            if late:
                started.append(copy)

    def merge(reducing):
        own = pltpu.make_async_copy(
            pieces.at[ring.me], landed.at[pl.ds(ring.slot(0, 0, 0) * tok, tok)], own_sem.at[0]
        )
        own.start()
        need(4)
        share = reducing.share
        came = set()

        def arrive(distance):
            if distance not in came:
                came.add(distance)
                for partner in partners:
                    if partner[1] == distance:
                        piece(*partner)[0].wait_recv()
                if distance == 0:
                    own.wait()

        def product(distance, s):
            arrive(distance)
            pick = []
            for other in (0, 1):
                for column in (0, 1):
                    if distance in (0, reach):
                        way, k = 0, column
                    else:
                        way, k = column, (column if s == 0 else 1 - column)
                    row = ring.slot(way, distance, other) * tok + k * part
                    pick.append(landed[row : row + part, :])
            x = jnp.concatenate(pick, axis=0)
            rows = ring.rows(distance, s)
            span = min(512, width)
            for j in range(width // span):
                cut = pl.ds(j * span, span)
                share[rows, cut] = narrow(
                    jnp.dot(x, weight[:, cut], preferred_element_type=jnp.float32)
                )
            reducing.start_pair(distance, s)

        last = reach - 1
        product(reach, 0)
        product(last, 0)
        reducing.finish_pair(reach, 0)
        reducing.launch(reach, False)
        product(last, 1)
        reducing.finish_pair(last, 0)
        reducing.launch(last, True)
        product(last - 1, 0)
        reducing.finish_pair(last, 1)
        for distance in range(last, 0, -1):
            if distance > 1:
                product(distance - 1, 1)
                reducing.finish_pair(distance - 1, 0)
            else:
                product(0, 0)
            reducing.step(distance, False)
            if distance > 1:
                if distance > 2:
                    product(distance - 2, 0)
                reducing.finish_pair(distance - 1, 1)
                reducing.step(distance - 1, True)
        reducing.finish_pair(0, 0)

    def scatter_pieces(values, at):
        for j in range(width // depth):
            pieces[at + j] = values[:, j * depth : (j + 1) * depth]

    def embed_pieces():
        need(1)
        scatter_pieces(normed(embed[...], embed_gain[...]), width // depth)

    first_sends()
    need(0)
    reducing = Reduce(ring, reduce1, started)
    layer(gather1, 0, reducing, (2, 3), gu1, down1, embed_pieces)
    send_pieces(0)
    first = narrow(wide(gather1[0][own_rows, :width]) + reducing.total())
    after_first[...] = first
    scatter_pieces(normed(first, hidden_gain[...]), 0)
    send_pieces(1)
    reducing = Reduce(ring, reduce2, started)
    merge(reducing)
    gather2[0][own_rows, :] = narrow(wide(after_first[...]) + jax.nn.silu(reducing.total()))
    for s in (0, 1):
        for way, k in streams(s):
            begin(ring_copy(gather2, way, 1, k))
        if s == 0:
            begin(sibling_copy(gather2, 0, 0, 0))
    reducing = Reduce(ring, reduce3, started)
    layer(gather2, 2, reducing, (5, 6), gu2, down2, lambda: None)
    out_ref[...] = narrow(wide(gather2[0][own_rows, :]) + reducing.total())
    for copy in started:
        copy.wait_send()


def fused(hidden_rows, token_embed, first_routes, first_gates, first_gate_up, first_down,
          second_routes, second_gates, second_gate_up, second_down, hidden_gain, embed_gain,
          merge_weight):
    devices = lax.axis_size("inner")
    tok, width = hidden_rows.shape
    hidden = first_down.shape[1]
    depth = merge_weight.shape[0]
    lanes = -(-4 * devices // LANES) * LANES
    vmem = pl.BlockSpec(memory_space=pltpu.VMEM)
    hbm = pl.BlockSpec(memory_space=pl.ANY)
    bf16 = jnp.bfloat16
    scratch = [
        pltpu.VMEM(first_gate_up.shape[1:], bf16),
        pltpu.VMEM(first_down.shape[1:], bf16),
        pltpu.VMEM(merge_weight.shape, bf16),
        pltpu.VMEM(second_gate_up.shape[1:], bf16),
        pltpu.VMEM(second_down.shape[1:], bf16),
        pltpu.SemaphoreType.DMA((7,)),
        pltpu.VMEM((lanes, -(-tok // LANES) * LANES), jnp.float32),
        pltpu.VMEM((tok, width), bf16),
        pltpu.VMEM((tok, width), bf16),
        pltpu.VMEM((devices, tok, depth), bf16),
        pltpu.VMEM((devices * tok, depth), bf16),
        pltpu.VMEM((4 * tok, hidden), bf16),
        pltpu.SemaphoreType.DMA((devices,)),
        pltpu.SemaphoreType.DMA((devices,)),
        pltpu.SemaphoreType.DMA((1,)),
        pltpu.SemaphoreType.DMA((4,)),
        pltpu.SemaphoreType.DMA((1,)),
    ]
    scratch += gather_scratch(devices, tok, width + lanes) + gather_scratch(devices, tok, width)
    for _ in range(3):
        scratch += reduce_scratch(devices, tok, width)
    return pl.pallas_call(
        functools.partial(block_kernel, devices),
        out_shape=jax.ShapeDtypeStruct((tok, width), bf16),
        in_specs=[vmem] * 6 + [hbm] * 7,
        out_specs=vmem,
        scratch_shapes=scratch,
        compiler_params=pltpu.CompilerParams(
            collective_id=0, has_side_effects=True, vmem_limit_bytes=VMEM_LIMIT
        ),
    )(first_routes.T, first_gates.T, second_routes.T, second_gates.T, hidden_gain[None],
      embed_gain[None], hidden_rows, token_embed, first_gate_up, first_down, merge_weight,
      second_gate_up, second_down)


def rms_scale(values, gain_vec):
    widened = values.astype(jnp.float32)
    inverse_rms = lax.rsqrt(jnp.mean(widened * widened, axis=-1, keepdims=True) + EPSILON)
    return (widened * inverse_rms * gain_vec).astype(jnp.bfloat16)


def dense_gates(routes, gates, experts):
    hit = routes[:, :, None] == jnp.arange(experts, dtype=jnp.int32)[None, None, :]
    return jnp.sum(jnp.where(hit, gates[:, :, None], 0.0), axis=1)


def plain_layer(devices, rows, routes, gates, gate_up, down):
    dense = lax.all_gather(dense_gates(routes, gates, devices), "inner", axis=0, tiled=True)
    column = lax.dynamic_slice_in_dim(dense, lax.axis_index("inner"), 1, axis=1)
    everyone = lax.all_gather(rows, "inner", axis=0, tiled=True)
    width = down.shape[1]
    projected = jnp.dot(everyone, gate_up[0], preferred_element_type=jnp.float32)
    inner = narrow(jax.nn.silu(projected[:, :width]) * projected[:, width:])
    share = narrow(jnp.dot(inner, down[0], preferred_element_type=jnp.float32) * column)
    total = lax.psum_scatter(share, "inner", scatter_dimension=0, tiled=True)
    return narrow(wide(rows) + wide(total))


def plain_merge(after_first, merged_in, weight):
    columns = lax.all_to_all(merged_in, "inner", split_axis=1, concat_axis=0, tiled=True)
    partial = narrow(jnp.dot(columns, weight, preferred_element_type=jnp.float32))
    merged = lax.psum_scatter(partial, "inner", scatter_dimension=0, tiled=True)
    return narrow(wide(after_first) + jax.nn.silu(wide(merged)))


def unfused(hidden_rows, token_embed, first_routes, first_gates, first_gate_up, first_down,
            second_routes, second_gates, second_gate_up, second_down, hidden_gain, embed_gain,
            merge_weight):
    devices = lax.axis_size("inner")
    after_first = plain_layer(
        devices, hidden_rows, first_routes, first_gates, first_gate_up, first_down
    )
    merged_in = jnp.concatenate(
        [rms_scale(after_first, hidden_gain), rms_scale(token_embed, embed_gain)], axis=1
    )
    after_merge = plain_merge(after_first, merged_in, merge_weight)
    return plain_layer(devices, after_merge, second_routes, second_gates, second_gate_up, second_down)


def local(hidden_rows, *others):
    devices = lax.axis_size("inner")
    tok, width = hidden_rows.shape
    fits = (
        12 * devices * tok * width * 2 <= VMEM_LIMIT
        and devices % 4 == 0 and devices >= 16 and tok % 32 == 0
    )
    return (fused if fits else unfused)(hidden_rows, *others)


def solution(mesh):
    rows = P(("groups", "inner"), None)
    return jax.shard_map(
        local,
        mesh=mesh,
        in_specs=(
            rows, rows, rows, rows,
            P("inner", None, None),
            P("inner", None, None),
            rows, rows,
            P("inner", None, None),
            P("inner", None, None),
            P(),
            P(),
            P("inner", None),
        ),
        out_specs=rows,
        check_vma=False,
    )
```

time: 154 us -> 139 us (0.903)
  Pallas kernels: 146 us -> 137 us
  local copies, waits for them, and re-layouts: 7.17 us -> 1.67 us
    pallas_call x1, Pallas kernels: 146 us -> 137 us  [fused(): pl.pallas_call(functools.partial(block_kernel, devices), out_shape=jax.Sh...]
    unnamed x5 -> x1, local copies, waits for them, and re-layouts: 7.17 us -> 1.67 us
where the time goes in v1:
time: 139 us; the launch traced here: 138 us
  Pallas kernels  137 us (99%)
  local copies, waits for them, and re-layouts  1.67 us (1%)
    pallas_call x1, Pallas kernels, fused(): pl.pallas_call(functools.partial(block_kernel, devices), out_shape=jax.Sh...  137 us

profile of v1, /device:TPU:0, one launch (start us, length us, event | category | flops | bytes accessed | tf_op | source)
XLA Modules:
  0.0 138.5 jit_solution(13562340202831238040)
XLA Ops:
  0.0 136.8 %shard_map.127 = bf16[64,2048]{1,0:T(8,128)(2,1)} custom-call(s32[8,64]{1,0:T(8,128)} %bitcast.8, f32[8,64]{1,0:T(8,128)} %bitcast.9, s32[8,64]{1,0:T(8,128)} %bitcast.10, f32[8,64]{1,0:T(8,128)} %bitcast.11, f32[1,2048]{1,0:T(1,128)} %bitcast.6, f32[1,2048]{1,0:T(1,128)} %bitcast.7, bf16[64,2048]{1,0:T(8,128)(2,1)} %refs_6_.1, bf16[64,2048]{1,0:T(8,128)(2,1)} %refs_7_.1, ...), custom_call_target="tpu_custom_call" | custom-call | tf_op jit(solution)/shard_map/pallas_call | solution.py:573
  136.8 1.7 %copy.15 = bf16[64,2048]{1,0:T(8,128)(2,1)} copy(bf16[64,2048]{1,0:T(8,128)(2,1)} %shard_map.127) | data formatting | bytes 524288

commit v2 on v1

--- a/solution.py
+++ b/solution.py
@@ -9,7 +9,7 @@
 
 EPSILON = 1e-06
 LANES = 128
-CUTS = 2
+CUTS = 4
 VMEM_LIMIT = 60 * 1024 * 1024
 
 
@@ -59,6 +59,11 @@
             s, column = (0 if k == way else 1), way
         return pl.ds(self.first(distance, s) + other * self.tok + column * part, part)
 
+    def chunk(self, way, distance, k):
+        if distance == self.reach:
+            return way
+        return 2 + (way * (self.reach - 1) + distance - 1) * 2 + k
+
     def slot(self, way, distance, other):
         if distance == 0:
             return (self.reach - 1) * 4 + 2 + other
@@ -82,11 +87,15 @@
     return values.astype(jnp.bfloat16)
 
 
+def sent(ring, whole, sem):
+    remote(whole, whole, sem, sem, ring.device(0, 1)).wait_send()
+
+
 class Reduce:
-    def __init__(self, ring, bufs, started):
-        self.ring, self.started = ring, started
-        (self.share, self.paired, self.arrived, self.pair_send, self.pair_recv, self.send,
-         self.recv) = bufs
+    def __init__(self, ring, bufs, recvs):
+        self.ring = ring
+        self.share, self.paired, self.arrived, self.send = bufs
+        self.pair_recv, self.recv = recvs
         self.cut = self.share.shape[1] // CUTS
 
     def pair_copy(self, distance, s):
@@ -95,15 +104,11 @@
         here = self.paired.at[pl.ds(slot * ring.tok, ring.tok)]
         return remote(
             self.share.at[ring.side(distance, s, 1)], here,
-            self.pair_send.at[slot], self.pair_recv.at[slot], ring.device(0, 1),
+            self.send.at[0], self.pair_recv.at[slot], ring.device(0, 1),
         ), here
 
-    def begin(self, copy):
-        copy.start()
-        self.started.append(copy)
-
     def start_pair(self, distance, s):
-        self.begin(self.pair_copy(distance, s)[0])
+        self.pair_copy(distance, s)[0].start()
 
     def finish_pair(self, distance, s):
         copy, here = self.pair_copy(distance, s)
@@ -117,18 +122,18 @@
     def hop(self, way, distance, k, c):
         ring = self.ring
         rows = ring.tok // 2
-        slot = (way * ring.reach + distance - 1) * 2 + k
+        slot = ring.chunk(way, distance, k)
         landing = self.arrived.at[pl.ds(slot * rows, rows), self.columns(c)]
         return remote(
             self.share.at[ring.half(1 - way, distance, 0, k), self.columns(c)], landing,
-            self.send.at[slot * CUTS + c], self.recv.at[slot * CUTS + c],
+            self.send.at[1], self.recv.at[slot * CUTS + c],
             ring.device(1 - 2 * way, 0),
         ), landing
 
     def launch(self, distance, flip):
         for c in range(CUTS):
             for way in (0, 1):
-                self.begin(self.hop(way, distance, 1 - way if flip else way, c)[0])
+                self.hop(way, distance, 1 - way if flip else way, c)[0].start()
 
     def step(self, distance, flip):
         for c in range(CUTS):
@@ -138,7 +143,12 @@
                 copy.wait_recv()
                 at = (self.ring.half(1 - way, distance, 0, k), self.columns(c))
                 self.share[at] = narrow(wide(self.share[at]) + wide(landing[...]))
-                self.begin(self.hop(way, distance, k, c)[0])
+                self.hop(way, distance, k, c)[0].start()
+
+    def drain(self):
+        ring = self.ring
+        sent(ring, self.share.at[pl.ds(0, 2 * ring.reach * ring.tok)], self.send.at[0])
+        sent(ring, self.share.at[pl.ds(0, (2 * ring.reach - 1) * ring.tok)], self.send.at[1])
 
     def total(self):
         parts = []
@@ -160,22 +170,23 @@
     return [
         pltpu.VMEM((devices * tok, width), jnp.bfloat16),
         pltpu.VMEM((2 * reach * tok, width), jnp.bfloat16),
-        pltpu.VMEM((2 * reach * tok, width), jnp.bfloat16),
-        pltpu.SemaphoreType.DMA((2 * reach,)),
-        pltpu.SemaphoreType.DMA((2 * reach,)),
-        pltpu.SemaphoreType.DMA((4 * reach * CUTS,)),
-        pltpu.SemaphoreType.DMA((4 * reach * CUTS,)),
+        pltpu.VMEM(((2 * reach - 1) * tok, width), jnp.bfloat16),
+        pltpu.SemaphoreType.DMA((2,)),
     ]
 
 
-def gather_scratch(devices, tok, width):
+def reduce_recvs(devices):
     reach = devices // 4
     return [
+        pltpu.SemaphoreType.DMA((2 * reach,)),
+        pltpu.SemaphoreType.DMA(((4 * reach - 2) * CUTS,)),
+    ]
+
+
+def gather_scratch(devices, tok, width):
+    return [
         pltpu.VMEM((devices * tok, width), jnp.bfloat16),
-        pltpu.SemaphoreType.DMA((4 * reach,)),
-        pltpu.SemaphoreType.DMA((4 * reach,)),
-        pltpu.SemaphoreType.DMA((4 * reach + 1,)),
-        pltpu.SemaphoreType.DMA((4 * reach + 1,)),
+        pltpu.SemaphoreType.DMA((2,)),
     ]
 
 
@@ -207,9 +218,10 @@
     take = lambda count: [scratch.pop(0) for _ in range(count)]
     gu1, down1, weight, gu2, down2, load_sem = take(6)
     turned, embed, after_first, pieces, landed, inner = take(6)
-    piece_send, piece_recv, own_sem, lane_send, lane_pair = take(5)
-    gather1, gather2 = take(5), take(5)
-    reduce1, reduce2, reduce3 = take(7), take(7), take(7)
+    piece_send, piece_recv, own_sem, ring_recv, sib_recv = take(5)
+    gather1, gather2 = take(2), take(2)
+    reduce1, reduce2, reduce3 = take(4), take(4), take(4)
+    recvs1, recvs2 = take(2), take(2)
     tok, width = hidden_ref.shape
     hidden = down1.shape[0]
     depth = weight.shape[0]
@@ -241,12 +253,8 @@
                 waiting.remove(i)
                 loads[i].wait()
 
-    pl.semaphore_wait(barrier, len(neighbours))
-    started = []
-
     def begin(copy):
         copy.start()
-        started.append(copy)
 
     partners = [(0, 0, 1)]
     for distance in range(1, reach + 1):
@@ -259,65 +267,63 @@
         return [(way, 1 - way if s else way) for way in (0, 1)]
 
     def ring_copy(bufs, way, distance, k):
-        everyone, send, recv = bufs[:3]
-        slot = (way * reach + distance - 1) * 2 + k
+        everyone, send = bufs
+        slot = ring.chunk(way, distance, k)
         if distance == 1:
             origin = everyone.at[ring.half(way, 0, 0, k)]
         else:
             origin = everyone.at[ring.half(way, distance - 1, 0, k)]
         return remote(
-            origin, everyone.at[ring.half(way, distance, 0, k)], send.at[slot], recv.at[slot],
+            origin, everyone.at[ring.half(way, distance, 0, k)], send.at[0], ring_recv.at[slot],
             ring.device(1 - 2 * way, 0),
         )
 
     def sibling_copy(bufs, way, distance, k):
-        everyone, sib_send, sib_recv = bufs[0], bufs[3], bufs[4]
+        everyone, send = bufs
         if distance == 0:
-            slot, origin, landing = 4 * reach, own_rows, ring.side(0, 0, 1)
+            s, origin, landing = 0, own_rows, ring.side(0, 0, 1)
         else:
-            slot = (way * reach + distance - 1) * 2 + k
+            s = 0 if distance == reach or k == way else 1
             origin, landing = ring.half(way, distance, 0, k), ring.half(way, distance, 1, k)
         return remote(
-            everyone.at[origin], everyone.at[landing], sib_send.at[slot], sib_recv.at[slot],
-            ring.device(0, 1),
+            everyone.at[origin], everyone.at[landing], send.at[1],
+            sib_recv.at[ring.spans.index((distance, s))], ring.device(0, 1),
         )
 
     def first_sends():
-        everyone, send, recv, sib_send, sib_recv = gather1
+        everyone, send = gather1
         narrow_cut, lane_cut = pl.ds(0, width), pl.ds(width, lanes)
 
         def send_rows(way, k):
-            slot = way * reach * 2 + k
             return remote(
                 hidden_ref.at[pl.ds(k * part, part)],
                 everyone.at[ring.half(way, 1, 0, k), narrow_cut],
-                send.at[slot], recv.at[slot], ring.device(1 - 2 * way, 0),
+                send.at[0], ring_recv.at[ring.chunk(way, 1, k)], ring.device(1 - 2 * way, 0),
             )
 
         def send_lanes(way, k):
-            slot = way * reach * 2 + k
             return remote(
                 everyone.at[ring.half(way, 0, 0, k), lane_cut],
                 everyone.at[ring.half(way, 1, 0, k), lane_cut],
-                lane_send.at[way * 2 + k], recv.at[slot], ring.device(1 - 2 * way, 0),
+                send.at[0], ring_recv.at[ring.chunk(way, 1, k)], ring.device(1 - 2 * way, 0),
             )
 
-        for way, k in streams(0):
-            begin(send_rows(way, k))
-        begin(remote(
-            hidden_ref, everyone.at[ring.side(0, 0, 1), narrow_cut],
-            sib_send.at[4 * reach], sib_recv.at[4 * reach], ring.device(0, 1),
-        ))
         for load in loads:
             load.start()
         everyone[own_rows, lane_cut] = gate_lanes(
             devices, turned, [(routes1[...], gates1[...]), (routes2[...], gates2[...])]
         )
+        pl.semaphore_wait(barrier, len(neighbours))
         for way, k in streams(0):
+            begin(send_rows(way, k))
             begin(send_lanes(way, k))
         begin(remote(
+            hidden_ref, everyone.at[ring.side(0, 0, 1), narrow_cut],
+            send.at[1], sib_recv.at[0], ring.device(0, 1),
+        ))
+        begin(remote(
             everyone.at[own_rows, lane_cut], everyone.at[ring.side(0, 0, 1), lane_cut],
-            lane_pair.at[0], sib_recv.at[4 * reach], ring.device(0, 1),
+            send.at[1], sib_recv.at[0], ring.device(0, 1),
         ))
         for way, k in streams(1):
             begin(send_rows(way, k))
@@ -338,11 +344,11 @@
                 begin(sibling_copy(bufs, way, distance, k))
 
         def from_sibling(distance, s):
-            if distance == 0:
-                sibling_copy(bufs, 0, 0, 0).wait_recv()
-            else:
-                for way, k in streams(s):
-                    sibling_copy(bufs, way, distance, k).wait_recv()
+            both = bufs[0].at[ring.side(distance, s, 1)]
+            remote(
+                both, both, bufs[1].at[1], sib_recv.at[ring.spans.index((distance, s))],
+                ring.device(0, 1),
+            ).wait_recv()
 
         def up(first_row, count, low, high):
             rows = pl.ds(first_row, count)
@@ -381,9 +387,9 @@
         need(load_ids[0])
         up(near, 2 * tok, 0, steps)
         need(load_ids[1])
+        pass_on(1, 0)
         finish(near, 2 * tok, (0, 0))
         meanwhile()
-        pass_on(1, 0)
         for distance in range(1, reach - 1):
             pass_on(distance, 1)
             from_sibling(distance, 0)
@@ -428,7 +434,7 @@
         slot = ring.slot(way, distance, other)
         return remote(
             pieces.at[target], landed.at[pl.ds(slot * tok, tok)],
-            piece_send.at[slot], piece_recv.at[slot], target,
+            piece_send.at[0], piece_recv.at[distance], target,
         ), target * depth >= width
 
     def send_pieces(late):
@@ -438,9 +444,6 @@
             @pl.when(embedded if late == 0 else jnp.logical_not(embedded))
             def _():
                 copy.start()
-
-            if late:
-                started.append(copy)
 
     def merge(reducing):
         own = pltpu.make_async_copy(
@@ -454,9 +457,12 @@
         def arrive(distance):
             if distance not in came:
                 came.add(distance)
-                for partner in partners:
-                    if partner[1] == distance:
-                        piece(*partner)[0].wait_recv()
+                low = min(ring.slot(*p) for p in partners if p[1] == distance)
+                count = sum(p[1] == distance for p in partners)
+                whole = landed.at[pl.ds(low * tok, count * tok)]
+                remote(
+                    whole, whole, piece_send.at[0], piece_recv.at[distance], ring.device(0, 1)
+                ).wait_recv()
                 if distance == 0:
                     own.wait()
 
@@ -515,14 +521,14 @@
 
     first_sends()
     need(0)
-    reducing = Reduce(ring, reduce1, started)
+    reducing1 = reducing = Reduce(ring, reduce1, recvs1)
     layer(gather1, 0, reducing, (2, 3), gu1, down1, embed_pieces)
     send_pieces(0)
     first = narrow(wide(gather1[0][own_rows, :width]) + reducing.total())
     after_first[...] = first
     scatter_pieces(normed(first, hidden_gain[...]), 0)
     send_pieces(1)
-    reducing = Reduce(ring, reduce2, started)
+    reducing2 = reducing = Reduce(ring, reduce2, recvs2)
     merge(reducing)
     gather2[0][own_rows, :] = narrow(wide(after_first[...]) + jax.nn.silu(reducing.total()))
     for s in (0, 1):
@@ -530,11 +536,15 @@
             begin(ring_copy(gather2, way, 1, k))
         if s == 0:
             begin(sibling_copy(gather2, 0, 0, 0))
-    reducing = Reduce(ring, reduce3, started)
+    reducing3 = reducing = Reduce(ring, reduce3, recvs2)
     layer(gather2, 2, reducing, (5, 6), gu2, down2, lambda: None)
     out_ref[...] = narrow(wide(gather2[0][own_rows, :]) + reducing.total())
-    for copy in started:
-        copy.wait_send()
+    for everyone, send in (gather1, gather2):
+        sent(ring, everyone.at[pl.ds(0, (2 * reach - 1) * tok)], send.at[0])
+        sent(ring, everyone.at[pl.ds(0, 2 * reach * tok)], send.at[1])
+    sent(ring, landed.at[pl.ds(0, (devices - 1) * tok)], piece_send.at[0])
+    for each in (reducing1, reducing2, reducing3):
+        each.drain()
 
 
 def fused(hidden_rows, token_embed, first_routes, first_gates, first_gate_up, first_down,
@@ -545,6 +555,7 @@
     hidden = first_down.shape[1]
     depth = merge_weight.shape[0]
     lanes = -(-4 * devices // LANES) * LANES
+    reach = devices // 4
     vmem = pl.BlockSpec(memory_space=pltpu.VMEM)
     hbm = pl.BlockSpec(memory_space=pl.ANY)
     bf16 = jnp.bfloat16
@@ -561,15 +572,16 @@
         pltpu.VMEM((devices, tok, depth), bf16),
         pltpu.VMEM((devices * tok, depth), bf16),
         pltpu.VMEM((4 * tok, hidden), bf16),
-        pltpu.SemaphoreType.DMA((devices,)),
-        pltpu.SemaphoreType.DMA((devices,)),
         pltpu.SemaphoreType.DMA((1,)),
-        pltpu.SemaphoreType.DMA((4,)),
+        pltpu.SemaphoreType.DMA((reach + 1,)),
         pltpu.SemaphoreType.DMA((1,)),
+        pltpu.SemaphoreType.DMA((4 * reach - 2,)),
+        pltpu.SemaphoreType.DMA((2 * reach,)),
     ]
     scratch += gather_scratch(devices, tok, width + lanes) + gather_scratch(devices, tok, width)
     for _ in range(3):
         scratch += reduce_scratch(devices, tok, width)
+    scratch += reduce_recvs(devices) + reduce_recvs(devices)
     return pl.pallas_call(
         functools.partial(block_kernel, devices),
         out_shape=jax.ShapeDtypeStruct((tok, width), bf16),

time: 139 us -> 134 us (0.964)
  Pallas kernels: 137 us -> 132 us
    pallas_call x1, Pallas kernels: 137 us -> 132 us  [fused(): pl.pallas_call(functools.partial(block_kernel, devices), out_shape=jax.Sh...]
where the time goes in v2:
time: 134 us
  Pallas kernels  132 us (99%)
  local copies, waits for them, and re-layouts  1.67 us (1%)
    pallas_call x1, Pallas kernels, fused(): pl.pallas_call(functools.partial(block_kernel, devices), out_shape=jax.Sh...  132 us

profile of v2, /device:TPU:0, one launch (start us, length us, event | category | flops | bytes accessed | tf_op | source)
XLA Modules:
  0.0 133.5 jit_solution(348759586988468297)
XLA Ops:
  0.0 131.9 %shard_map.127 = bf16[64,2048]{1,0:T(8,128)(2,1)} custom-call(s32[8,64]{1,0:T(8,128)} %bitcast.8, f32[8,64]{1,0:T(8,128)} %bitcast.9, s32[8,64]{1,0:T(8,128)} %bitcast.10, f32[8,64]{1,0:T(8,128)} %bitcast.11, f32[1,2048]{1,0:T(1,128)} %bitcast.6, f32[1,2048]{1,0:T(1,128)} %bitcast.7, bf16[64,2048]{1,0:T(8,128)(2,1)} %refs_6_.1, bf16[64,2048]{1,0:T(8,128)(2,1)} %refs_7_.1, ...), custom_call_target="tpu_custom_call" | custom-call | tf_op jit(solution)/shard_map/pallas_call | solution.py:585
  131.9 1.7 %copy.15 = bf16[64,2048]{1,0:T(8,128)(2,1)} copy(bf16[64,2048]{1,0:T(8,128)(2,1)} %shard_map.127) | data formatting | bytes 524288

commit v3 on v2

--- a/solution.py
+++ b/solution.py
@@ -135,8 +135,8 @@
             for way in (0, 1):
                 self.hop(way, distance, 1 - way if flip else way, c)[0].start()
 
-    def step(self, distance, flip):
-        for c in range(CUTS):
+    def step(self, distance, flip, cuts=range(CUTS)):
+        for c in cuts:
             for way in (0, 1):
                 k = 1 - way if flip else way
                 copy, landing = self.hop(way, distance + 1, k, c)
@@ -150,19 +150,19 @@
         sent(ring, self.share.at[pl.ds(0, 2 * ring.reach * ring.tok)], self.send.at[0])
         sent(ring, self.share.at[pl.ds(0, (2 * ring.reach - 1) * ring.tok)], self.send.at[1])
 
+    def piece(self, c):
+        halves = []
+        for k in (0, 1):
+            piece = wide(self.share[self.ring.half(0, 0, 0, k), self.columns(c)])
+            for way in (0, 1):
+                copy, landing = self.hop(way, 1, k, c)
+                copy.wait_recv()
+                piece = piece + wide(landing[...])
+            halves.append(piece)
+        return jnp.concatenate(halves, axis=0)
+
     def total(self):
-        parts = []
-        for c in range(CUTS):
-            halves = []
-            for k in (0, 1):
-                piece = wide(self.share[self.ring.half(0, 0, 0, k), self.columns(c)])
-                for way in (0, 1):
-                    copy, landing = self.hop(way, 1, k, c)
-                    copy.wait_recv()
-                    piece = piece + wide(landing[...])
-                halves.append(piece)
-            parts.append(jnp.concatenate(halves, axis=0))
-        return jnp.concatenate(parts, axis=1)
+        return jnp.concatenate([self.piece(c) for c in range(CUTS)], axis=1)
 
 
 def reduce_scratch(devices, tok, width):
@@ -266,15 +266,14 @@
     def streams(s):
         return [(way, 1 - way if s else way) for way in (0, 1)]
 
-    def ring_copy(bufs, way, distance, k):
+    def ring_copy(bufs, way, distance, k, cut=None):
         everyone, send = bufs
         slot = ring.chunk(way, distance, k)
-        if distance == 1:
-            origin = everyone.at[ring.half(way, 0, 0, k)]
-        else:
-            origin = everyone.at[ring.half(way, distance - 1, 0, k)]
+        rows = ring.half(way, max(distance - 1, 0), 0, k)
+        landing = ring.half(way, distance, 0, k)
+        cut = pl.ds(0, everyone.shape[1]) if cut is None else cut
         return remote(
-            origin, everyone.at[ring.half(way, distance, 0, k)], send.at[0], ring_recv.at[slot],
+            everyone.at[rows, cut], everyone.at[landing, cut], send.at[0], ring_recv.at[slot],
             ring.device(1 - 2 * way, 0),
         )
 
@@ -353,10 +352,8 @@
         def up(first_row, count, low, high):
             rows = pl.ds(first_row, count)
 
-            @pl.loop(low, high)
-            def _(j):
-                left = pl.ds(pl.multiple_of(j * step, step), step)
-                right = pl.ds(pl.multiple_of(hidden + j * step, step), step)
+            for j in range(low, high):
+                left, right = pl.ds(j * step, step), pl.ds(hidden + j * step, step)
                 x = everyone[rows, :width]
                 g = jnp.dot(x, gu[:, left], preferred_element_type=jnp.float32)
                 u = jnp.dot(x, gu[:, right], preferred_element_type=jnp.float32)
@@ -371,9 +368,8 @@
             )
             span = min(512, width)
 
-            @pl.loop(0, width // span)
-            def _(j):
-                cut = pl.ds(pl.multiple_of(j * span, span), span)
+            for j in range(width // span):
+                cut = pl.ds(j * span, span)
                 out = jnp.dot(
                     inner[:count, :], down[:, cut], preferred_element_type=jnp.float32
                 )
@@ -382,42 +378,33 @@
             for at in spans:
                 reducing.start_pair(*at)
 
-        near = ring.first(0, 0)
+        last = reach - 1
+        spans = ring.spans
         from_sibling(0, 0)
         need(load_ids[0])
-        up(near, 2 * tok, 0, steps)
+        up(ring.first(0, 0), 2 * tok, 0, steps)
+        pass_on(1, 0)
         need(load_ids[1])
-        pass_on(1, 0)
-        finish(near, 2 * tok, (0, 0))
+        finish(ring.first(0, 0), 2 * tok, (0, 0))
         meanwhile()
-        for distance in range(1, reach - 1):
-            pass_on(distance, 1)
-            from_sibling(distance, 0)
-            from_sibling(distance, 1)
-            up(ring.first(distance, 0), 4 * tok, 0, steps // 2)
-            pass_on(distance + 1, 0)
-            up(ring.first(distance, 0), 4 * tok, steps // 2, steps)
-            finish(ring.first(distance, 0), 4 * tok, (distance, 0), (distance, 1))
-            if distance == 1:
-                reducing.finish_pair(0, 0)
-            else:
-                reducing.finish_pair(distance - 1, 0)
-                reducing.finish_pair(distance - 1, 1)
-        last = reach - 1
-        pass_on(last, 1)
-        from_sibling(last, 0)
-        up(ring.first(last, 0), 2 * tok, 0, steps)
-        finish(ring.first(last, 0), 2 * tok, (last, 0))
-        pass_on(reach, 0)
-        from_sibling(last, 1)
-        reducing.finish_pair(last, 0)
-        reducing.launch(last, True)
+        for at, span in enumerate(spans[1:-1], 1):
+            from_sibling(*span)
+            up(ring.first(*span), 2 * tok, 0, steps // 2)
+            if span == (last, 1):
+                reducing.finish_pair(last, 0)
+                reducing.launch(last, True)
+            up(ring.first(*span), 2 * tok, steps // 2, steps)
+            pass_on(*spans[at + 1])
+            finish(ring.first(*span), 2 * tok, span)
+            if span != (last, 1):
+                reducing.finish_pair(*spans[at - 1])
         from_sibling(reach, 0)
-        up(ring.first(last, 1), 4 * tok, 0, steps)
-        finish(ring.first(last, 1), 4 * tok, (reach, 0), (last, 1))
-        reducing.finish_pair(last - 1, 0)
-        reducing.finish_pair(last - 1, 1)
-        reducing.step(last - 1, True)
+        up(ring.first(reach, 0), 2 * tok, 0, steps // 2)
+        reducing.step(last - 1, True, range(0, 1))
+        up(ring.first(reach, 0), 2 * tok, steps // 2, steps)
+        reducing.step(last - 1, True, range(1, CUTS - 1))
+        finish(ring.first(reach, 0), 2 * tok, (reach, 0))
+        reducing.step(last - 1, True, range(CUTS - 1, CUTS))
         reducing.finish_pair(reach, 0)
         reducing.launch(reach, False)
         reducing.finish_pair(last, 1)
@@ -435,15 +422,11 @@
         return remote(
             pieces.at[target], landed.at[pl.ds(slot * tok, tok)],
             piece_send.at[0], piece_recv.at[distance], target,
-        ), target * depth >= width
-
-    def send_pieces(late):
+        )
+
+    def send_pieces():
         for partner in reversed(partners):
-            copy, embedded = piece(*partner)
-
-            @pl.when(embedded if late == 0 else jnp.logical_not(embedded))
-            def _():
-                copy.start()
+            begin(piece(*partner))
 
     def merge(reducing):
         own = pltpu.make_async_copy(
@@ -523,19 +506,23 @@
     need(0)
     reducing1 = reducing = Reduce(ring, reduce1, recvs1)
     layer(gather1, 0, reducing, (2, 3), gu1, down1, embed_pieces)
-    send_pieces(0)
     first = narrow(wide(gather1[0][own_rows, :width]) + reducing.total())
     after_first[...] = first
     scatter_pieces(normed(first, hidden_gain[...]), 0)
-    send_pieces(1)
+    send_pieces()
     reducing2 = reducing = Reduce(ring, reduce2, recvs2)
     merge(reducing)
-    gather2[0][own_rows, :] = narrow(wide(after_first[...]) + jax.nn.silu(reducing.total()))
-    for s in (0, 1):
-        for way, k in streams(s):
-            begin(ring_copy(gather2, way, 1, k))
-        if s == 0:
-            begin(sibling_copy(gather2, 0, 0, 0))
+    everyone, send = gather2
+    for c in range(CUTS):
+        cut = reducing.columns(c)
+        everyone[own_rows, cut] = narrow(
+            wide(after_first[:, cut]) + jax.nn.silu(reducing.piece(c))
+        )
+        for way, k in streams(0):
+            begin(ring_copy(gather2, way, 1, k, cut))
+    for way, k in streams(1):
+        begin(ring_copy(gather2, way, 1, k))
+    begin(sibling_copy(gather2, 0, 0, 0))
     reducing3 = reducing = Reduce(ring, reduce3, recvs2)
     layer(gather2, 2, reducing, (5, 6), gu2, down2, lambda: None)
     out_ref[...] = narrow(wide(gather2[0][own_rows, :]) + reducing.total())

time: 134 us -> 129 us (0.963)
  Pallas kernels: 132 us -> 128 us
    pallas_call x1, Pallas kernels: 132 us -> 128 us  [fused(): pl.pallas_call(functools.partial(block_kernel, devices), out_shape=jax.Sh...]
where the time goes in v3:
time: 129 us
  Pallas kernels  128 us (99%)
  local copies, waits for them, and re-layouts  1.67 us (1%)
    pallas_call x1, Pallas kernels, fused(): pl.pallas_call(functools.partial(block_kernel, devices), out_shape=jax.Sh...  128 us

profile of v3, /device:TPU:0, one launch (start us, length us, event | category | flops | bytes accessed | tf_op | source)
XLA Modules:
  0.0 129.2 jit_solution(3754187945713212802)
XLA Ops:
  0.0 127.5 %shard_map.127 = bf16[64,2048]{1,0:T(8,128)(2,1)} custom-call(s32[8,64]{1,0:T(8,128)} %bitcast.8, f32[8,64]{1,0:T(8,128)} %bitcast.9, s32[8,64]{1,0:T(8,128)} %bitcast.10, f32[8,64]{1,0:T(8,128)} %bitcast.11, f32[1,2048]{1,0:T(1,128)} %bitcast.6, f32[1,2048]{1,0:T(1,128)} %bitcast.7, bf16[64,2048]{1,0:T(8,128)(2,1)} %refs_6_.1, bf16[64,2048]{1,0:T(8,128)(2,1)} %refs_7_.1, ...), custom_call_target="tpu_custom_call" | custom-call | tf_op jit(solution)/shard_map/pallas_call | solution.py:572
  127.5 1.7 %copy.15 = bf16[64,2048]{1,0:T(8,128)(2,1)} copy(bf16[64,2048]{1,0:T(8,128)(2,1)} %shard_map.127) | data formatting | bytes 524288

commit v4 on v3

--- a/solution.py
+++ b/solution.py
@@ -119,6 +119,25 @@
     def columns(self, c):
         return pl.ds(c * self.cut, self.cut)
 
+    def far_copy(self, c):
+        ring = self.ring
+        slot = 2 * ring.reach - 1
+        here = self.paired.at[pl.ds(slot * ring.tok, ring.tok), self.columns(c)]
+        return remote(
+            self.share.at[ring.side(ring.reach, 0, 1), self.columns(c)], here,
+            self.send.at[0], self.pair_recv.at[slot + c], ring.device(0, 1),
+        ), here
+
+    def launch_far(self):
+        ring = self.ring
+        for c in range(CUTS):
+            copy, here = self.far_copy(c)
+            copy.wait_recv()
+            at = (ring.side(ring.reach, 0, 0), self.columns(c))
+            self.share[at] = narrow(wide(self.share[at]) + wide(here[...]))
+            for way in (0, 1):
+                self.hop(way, ring.reach, way, c)[0].start()
+
     def hop(self, way, distance, k, c):
         ring = self.ring
         rows = ring.tok // 2
@@ -178,7 +197,7 @@
 def reduce_recvs(devices):
     reach = devices // 4
     return [
-        pltpu.SemaphoreType.DMA((2 * reach,)),
+        pltpu.SemaphoreType.DMA((2 * reach - 1 + CUTS,)),
         pltpu.SemaphoreType.DMA(((4 * reach - 2) * CUTS,)),
     ]
 
@@ -212,8 +231,8 @@
 
 
 def block_kernel(devices, *refs):
-    (routes1, gates1, routes2, gates2, hidden_gain, embed_gain, hidden_ref, embed_ref,
-     gu1_ref, down1_ref, weight_ref, gu2_ref, down2_ref, out_ref) = refs[:14]
+    smalls = refs[:6]
+    hidden_ref, embed_ref, gu1_ref, down1_ref, weight_ref, gu2_ref, down2_ref, out_ref = refs[6:14]
     scratch = list(refs[14:])
     take = lambda count: [scratch.pop(0) for _ in range(count)]
     gu1, down1, weight, gu2, down2, load_sem = take(6)
@@ -222,6 +241,8 @@
     gather1, gather2 = take(2), take(2)
     reduce1, reduce2, reduce3 = take(4), take(4), take(4)
     recvs1, recvs2 = take(2), take(2)
+    out, out_sem = take(2)
+    routes1, gates1, routes2, gates2, hidden_gain, embed_gain = held = take(6)
     tok, width = hidden_ref.shape
     hidden = down1.shape[0]
     depth = weight.shape[0]
@@ -242,9 +263,11 @@
         for i, (source, target) in enumerate(
             [(hidden_ref, gather1[0].at[own_rows, pl.ds(0, width)]), (embed_ref, embed),
              (gu1_ref.at[0], gu1), (down1_ref.at[0], down1), (weight_ref, weight),
-             (gu2_ref.at[0], gu2), (down2_ref.at[0], down2)]
+             (gu2_ref.at[0], gu2), (down2_ref.at[0], down2), *zip(smalls, held)]
         )
     ]
+    for load in loads[7:] + loads[:7]:
+        load.start()
     waiting = list(range(len(loads)))
 
     def need(*which):
@@ -307,8 +330,7 @@
                 send.at[0], ring_recv.at[ring.chunk(way, 1, k)], ring.device(1 - 2 * way, 0),
             )
 
-        for load in loads:
-            load.start()
+        need(*range(7, len(loads)))
         everyone[own_rows, lane_cut] = gate_lanes(
             devices, turned, [(routes1[...], gates1[...]), (routes2[...], gates2[...])]
         )
@@ -359,24 +381,25 @@
                 u = jnp.dot(x, gu[:, right], preferred_element_type=jnp.float32)
                 inner[:count, left] = narrow(jax.nn.silu(g) * u)
 
-        def finish(first_row, count, *spans):
-            rows = pl.ds(first_row, count)
+        def finish(span):
+            count = 2 * tok
+            rows = ring.rows(*span)
             lane = lax.broadcasted_iota(jnp.int32, (count, lanes), 1)
             mine = (lane == ring.me + first * devices) | (lane == ring.me + (first + 1) * devices)
             gate = jnp.sum(
                 jnp.where(mine, wide(gate_rows[rows, width:]), 0.0), axis=1, keepdims=True
             )
-            span = min(512, width)
-
-            for j in range(width // span):
-                cut = pl.ds(j * span, span)
+            for c in range(CUTS):
+                cut = reducing.columns(c)
                 out = jnp.dot(
                     inner[:count, :], down[:, cut], preferred_element_type=jnp.float32
                 )
                 share[rows, cut] = narrow(out * gate)
-
-            for at in spans:
-                reducing.start_pair(*at)
+                if span == (reach, 0):
+                    reducing.far_copy(c)[0].start()
+
+            if span != (reach, 0):
+                reducing.start_pair(*span)
 
         last = reach - 1
         spans = ring.spans
@@ -385,17 +408,16 @@
         up(ring.first(0, 0), 2 * tok, 0, steps)
         pass_on(1, 0)
         need(load_ids[1])
-        finish(ring.first(0, 0), 2 * tok, (0, 0))
+        finish((0, 0))
         meanwhile()
         for at, span in enumerate(spans[1:-1], 1):
-            from_sibling(*span)
-            up(ring.first(*span), 2 * tok, 0, steps // 2)
             if span == (last, 1):
                 reducing.finish_pair(last, 0)
                 reducing.launch(last, True)
-            up(ring.first(*span), 2 * tok, steps // 2, steps)
+            from_sibling(*span)
+            up(ring.first(*span), 2 * tok, 0, steps)
             pass_on(*spans[at + 1])
-            finish(ring.first(*span), 2 * tok, span)
+            finish(span)
             if span != (last, 1):
                 reducing.finish_pair(*spans[at - 1])
         from_sibling(reach, 0)
@@ -403,10 +425,9 @@
         reducing.step(last - 1, True, range(0, 1))
         up(ring.first(reach, 0), 2 * tok, steps // 2, steps)
         reducing.step(last - 1, True, range(1, CUTS - 1))
-        finish(ring.first(reach, 0), 2 * tok, (reach, 0))
+        finish((reach, 0))
         reducing.step(last - 1, True, range(CUTS - 1, CUTS))
-        reducing.finish_pair(reach, 0)
-        reducing.launch(reach, False)
+        reducing.launch_far()
         reducing.finish_pair(last, 1)
         for distance in range(last, 0, -1):
             if distance > 2:
@@ -462,19 +483,20 @@
                     pick.append(landed[row : row + part, :])
             x = jnp.concatenate(pick, axis=0)
             rows = ring.rows(distance, s)
-            span = min(512, width)
-            for j in range(width // span):
-                cut = pl.ds(j * span, span)
+            for c in range(CUTS):
+                cut = reducing.columns(c)
                 share[rows, cut] = narrow(
                     jnp.dot(x, weight[:, cut], preferred_element_type=jnp.float32)
                 )
-            reducing.start_pair(distance, s)
+                if distance == reach:
+                    reducing.far_copy(c)[0].start()
+            if distance != reach:
+                reducing.start_pair(distance, s)
 
         last = reach - 1
         product(reach, 0)
         product(last, 0)
-        reducing.finish_pair(reach, 0)
-        reducing.launch(reach, False)
+        reducing.launch_far()
         product(last, 1)
         reducing.finish_pair(last, 0)
         reducing.launch(last, True)
@@ -506,9 +528,16 @@
     need(0)
     reducing1 = reducing = Reduce(ring, reduce1, recvs1)
     layer(gather1, 0, reducing, (2, 3), gu1, down1, embed_pieces)
-    first = narrow(wide(gather1[0][own_rows, :width]) + reducing.total())
-    after_first[...] = first
-    scatter_pieces(normed(first, hidden_gain[...]), 0)
+    squares = jnp.zeros((tok, 1), jnp.float32)
+    for c in range(CUTS):
+        cut = reducing.columns(c)
+        first = narrow(wide(gather1[0][own_rows, cut]) + reducing.piece(c))
+        after_first[:, cut] = first
+        squares = squares + jnp.sum(wide(first) * wide(first), axis=-1, keepdims=True)
+    inverse_rms = lax.rsqrt(squares / width + EPSILON)
+    for j in range(width // depth):
+        cut = pl.ds(j * depth, depth)
+        pieces[j] = narrow(wide(after_first[:, cut]) * inverse_rms * hidden_gain[:, cut])
     send_pieces()
     reducing2 = reducing = Reduce(ring, reduce2, recvs2)
     merge(reducing)
@@ -525,13 +554,20 @@
     begin(sibling_copy(gather2, 0, 0, 0))
     reducing3 = reducing = Reduce(ring, reduce3, recvs2)
     layer(gather2, 2, reducing, (5, 6), gu2, down2, lambda: None)
-    out_ref[...] = narrow(wide(gather2[0][own_rows, :]) + reducing.total())
+    stores = []
+    for c in range(CUTS):
+        cut = reducing.columns(c)
+        out[:, cut] = narrow(wide(gather2[0][own_rows, cut]) + reducing.piece(c))
+        stores.append(pltpu.make_async_copy(out.at[:, cut], out_ref.at[:, cut], out_sem.at[c]))
+        stores[-1].start()
     for everyone, send in (gather1, gather2):
         sent(ring, everyone.at[pl.ds(0, (2 * reach - 1) * tok)], send.at[0])
         sent(ring, everyone.at[pl.ds(0, 2 * reach * tok)], send.at[1])
     sent(ring, landed.at[pl.ds(0, (devices - 1) * tok)], piece_send.at[0])
     for each in (reducing1, reducing2, reducing3):
         each.drain()
+    for store in stores:
+        store.wait()
 
 
 def fused(hidden_rows, token_embed, first_routes, first_gates, first_gate_up, first_down,
@@ -543,7 +579,6 @@
     depth = merge_weight.shape[0]
     lanes = -(-4 * devices // LANES) * LANES
     reach = devices // 4
-    vmem = pl.BlockSpec(memory_space=pltpu.VMEM)
     hbm = pl.BlockSpec(memory_space=pl.ANY)
     bf16 = jnp.bfloat16
     scratch = [
@@ -552,7 +587,7 @@
         pltpu.VMEM(merge_weight.shape, bf16),
         pltpu.VMEM(second_gate_up.shape[1:], bf16),
         pltpu.VMEM(second_down.shape[1:], bf16),
-        pltpu.SemaphoreType.DMA((7,)),
+        pltpu.SemaphoreType.DMA((13,)),
         pltpu.VMEM((lanes, -(-tok // LANES) * LANES), jnp.float32),
         pltpu.VMEM((tok, width), bf16),
         pltpu.VMEM((tok, width), bf16),
@@ -569,17 +604,20 @@
     for _ in range(3):
         scratch += reduce_scratch(devices, tok, width)
     scratch += reduce_recvs(devices) + reduce_recvs(devices)
+    scratch += [pltpu.VMEM((tok, width), bf16), pltpu.SemaphoreType.DMA((CUTS,))]
+    smalls = (first_routes.T, first_gates.T, second_routes.T, second_gates.T, hidden_gain[None],
+              embed_gain[None])
+    scratch += [pltpu.VMEM(small.shape, small.dtype) for small in smalls]
     return pl.pallas_call(
         functools.partial(block_kernel, devices),
         out_shape=jax.ShapeDtypeStruct((tok, width), bf16),
-        in_specs=[vmem] * 6 + [hbm] * 7,
-        out_specs=vmem,
+        in_specs=[hbm] * 13,
+        out_specs=hbm,
         scratch_shapes=scratch,
         compiler_params=pltpu.CompilerParams(
             collective_id=0, has_side_effects=True, vmem_limit_bytes=VMEM_LIMIT
         ),
-    )(first_routes.T, first_gates.T, second_routes.T, second_gates.T, hidden_gain[None],
-      embed_gain[None], hidden_rows, token_embed, first_gate_up, first_down, merge_weight,
+    )(*smalls, hidden_rows, token_embed, first_gate_up, first_down, merge_weight,
       second_gate_up, second_down)
 
 
@@ -632,7 +670,7 @@
     tok, width = hidden_rows.shape
     fits = (
         12 * devices * tok * width * 2 <= VMEM_LIMIT
-        and devices % 4 == 0 and devices >= 16 and tok % 32 == 0
+        and devices % 4 == 0 and devices >= 16 and tok % 32 == 0 and width % (CUTS * LANES) == 0
     )
     return (fused if fits else unfused)(hidden_rows, *others)
 

time: 129 us -> 128 us (level)
  Pallas kernels: 128 us -> 126 us
    pallas_call x1, Pallas kernels: 128 us -> 126 us  [fused(): pl.pallas_call(functools.partial(block_kernel, devices), out_shape=jax.Sh...]
where the time goes in v4:
time: 128 us; the launch traced here: 127 us
  Pallas kernels  126 us (98%)
  local copies, waits for them, and re-layouts  1.67 us (1%)
    pallas_call x1, Pallas kernels, fused(): pl.pallas_call(functools.partial(block_kernel, devices), out_shape=jax.Sh...  126 us

profile of v4, /device:TPU:0, one launch (start us, length us, event | category | flops | bytes accessed | tf_op | source)
XLA Modules:
  0.0 127.5 jit_solution(3591870699622593025)
XLA Ops:
  0.0 125.8 %shard_map.127 = bf16[64,2048]{1,0:T(8,128)(2,1)} custom-call(s32[8,64]{1,0:T(8,128)} %bitcast.8, f32[8,64]{1,0:T(8,128)} %bitcast.9, s32[8,64]{1,0:T(8,128)} %bitcast.10, f32[8,64]{1,0:T(8,128)} %bitcast.11, f32[1,2048]{1,0:T(1,128)} %bitcast.6, f32[1,2048]{1,0:T(1,128)} %bitcast.7, bf16[64,2048]{1,0:T(8,128)(2,1)} %refs_6_.1, bf16[64,2048]{1,0:T(8,128)(2,1)} %refs_7_.1, ...), custom_call_target="tpu_custom_call" | custom-call | tf_op jit(solution)/shard_map/pallas_call | solution.py:611
  125.8 1.7 %copy.15 = bf16[64,2048]{1,0:T(8,128)(2,1)} copy(bf16[64,2048]{1,0:T(8,128)(2,1)} %shard_map.127) | data formatting | bytes 524288

commit v5 on v4

--- a/solution.py
+++ b/solution.py
@@ -362,6 +362,7 @@
                 ring_copy(bufs, way, distance, k).wait_recv()
                 if distance + 1 < reach or (distance + 1 == reach and s == 0):
                     begin(ring_copy(bufs, way, distance + 1, k))
+            for way, k in streams(s):
                 begin(sibling_copy(bufs, way, distance, k))
 
         def from_sibling(distance, s):

time: 128 us -> 128 us (level)
  no operation moved by 1% of the time
where the time goes in v5:
time: 128 us; the launch traced here: 127 us
  Pallas kernels  126 us (98%)
  local copies, waits for them, and re-layouts  1.67 us (1%)
    pallas_call x1, Pallas kernels, fused(): pl.pallas_call(functools.partial(block_kernel, devices), out_shape=jax.Sh...  126 us

profile of v5, /device:TPU:0, one launch (start us, length us, event | category | flops | bytes accessed | tf_op | source)
XLA Modules:
  0.0 127.4 jit_solution(10834629204356689288)
XLA Ops:
  0.0 125.7 %shard_map.127 = bf16[64,2048]{1,0:T(8,128)(2,1)} custom-call(s32[8,64]{1,0:T(8,128)} %bitcast.8, f32[8,64]{1,0:T(8,128)} %bitcast.9, s32[8,64]{1,0:T(8,128)} %bitcast.10, f32[8,64]{1,0:T(8,128)} %bitcast.11, f32[1,2048]{1,0:T(1,128)} %bitcast.6, f32[1,2048]{1,0:T(1,128)} %bitcast.7, bf16[64,2048]{1,0:T(8,128)(2,1)} %refs_6_.1, bf16[64,2048]{1,0:T(8,128)(2,1)} %refs_7_.1, ...), custom_call_target="tpu_custom_call" | custom-call | tf_op jit(solution)/shard_map/pallas_call | solution.py:612
  125.7 1.7 %copy.15 = bf16[64,2048]{1,0:T(8,128)(2,1)} copy(bf16[64,2048]{1,0:T(8,128)(2,1)} %shard_map.127) | data formatting | bytes 524288
